TPU v7x, 32 devices: a whole 2x2x4 slice. The times are simulated.
32 devices in a mesh: fsdp: 2 (over x), ctx: 4 (over z), tp: 4 (over y, core).
Axes of the slice: x: 2, y: 2, z: 4, core: 2. Of those that a mesh axis runs over, the one named last changes fastest.
Arguments:
- tokens: bfloat16 [4, 2048, 2048], P('fsdp', 'ctx'), may hold values from -6 to 6
- tree_position: int32 [4, 2048], P('fsdp', 'ctx'), may hold values from 0 to 2047, as said below
- segment: int32 [4, 2048], P('fsdp', 'ctx'), may hold values from 0 to 6, as said below
- parent_table: int32 [4, 7], P('fsdp'), may hold values from 0 to 2, as said below
- norm1_gain: float32 [2048], replicated, may hold values from 0.5 to 1.5
- norm1_shift: float32 [2048], replicated, may hold values from -4 to 4
- query_weight: bfloat16 [2048, 2048], P('fsdp', 'tp'), may hold values from -0.125 to 0.125
- query_bias: float32 [2048], P('tp'), may hold values from -4 to 4
- key_weight: bfloat16 [2048, 2048], P('fsdp', 'tp'), may hold values from -0.125 to 0.125
- value_weight: bfloat16 [2048, 2048], P('fsdp', 'tp'), may hold values from -0.125 to 0.125
- value_bias: float32 [2048], P('tp'), may hold values from -0.75 to 0.75
- out_weight: bfloat16 [2048, 2048], P('tp', 'fsdp'), may hold values from -1.5 to 1.5
- out_bias: float32 [2048], replicated, may hold values from -4 to 4
- norm2_gain: float32 [2048], replicated, may hold values from 0.5 to 1.5
- norm2_shift: float32 [2048], replicated, may hold values from -4 to 4
- up_weight: bfloat16 [2048, 8192], P('fsdp', 'tp'), may hold values from -0.125 to 0.125
- up_bias: float32 [8192], P('tp'), may hold values from -4 to 4
- down_weight: bfloat16 [8192, 2048], P('tp', 'fsdp'), may hold values from -0.0625 to 0.0625
- down_bias: float32 [2048], replicated, may hold values from -4 to 4
- cotangent: bfloat16 [4, 2048, 2048], P('fsdp', 'ctx'), may hold values from -6 to 6
Outputs:
- layer_out: bfloat16 [4, 2048, 2048], P('fsdp', 'ctx')
- grad_tokens: bfloat16 [4, 2048, 2048], P('fsdp', 'ctx')
- grad_norm1_gain: float32 [2048], P(('fsdp', 'ctx'))
- grad_norm1_shift: float32 [2048], P(('fsdp', 'ctx'))
- grad_query_weight: float32 [2048, 2048], P(('fsdp', 'ctx'), 'tp')
- grad_query_bias: float32 [2048], P('tp')
- grad_key_weight: float32 [2048, 2048], P(('fsdp', 'ctx'), 'tp')
- grad_value_weight: float32 [2048, 2048], P(('fsdp', 'ctx'), 'tp')
- grad_value_bias: float32 [2048], P('tp')
- grad_out_weight: float32 [2048, 2048], P('tp', ('fsdp', 'ctx'))
- grad_out_bias: float32 [2048], P(('fsdp', 'ctx'))
- grad_norm2_gain: float32 [2048], P(('fsdp', 'ctx'))
- grad_norm2_shift: float32 [2048], P(('fsdp', 'ctx'))
- grad_up_weight: float32 [2048, 8192], P(('fsdp', 'ctx'), 'tp')
- grad_up_bias: float32 [8192], P('tp')
- grad_down_weight: float32 [8192, 2048], P('tp', ('fsdp', 'ctx'))
- grad_down_bias: float32 [2048], P(('fsdp', 'ctx'))
Inputs may be any that keep to these rules, and one draw needn't show every extreme that they name: `tree_position`: within each tree the rows hold the positions 0 to 2047 once each; every aligned run of 64 rows holds 64 consecutive positions in increasing order. `segment`: along increasing positions a tree runs through segments 0 to 6 in order, each nonempty and contiguous: the trunk 0 with 1024 positions, branches 1 and 2 with 512 together, leaves 3 to 6 with 512 together. `parent_table`: entry s of a tree's row is the parent of segment s: 0 for segments 0, 1 and 2; 1 for leaf 3; 2 for leaf 6; 1 or 2 for leaves 4 and 5.
All inputs are finite; a program needn't handle non-finite values.
Results may differ from a plain program's by a relative error of at most 0.024.
Values may be sent and summed in bfloat16 or wider, within the bound.
No kernel may reach another device: no remote copies, remote signals or barrier semaphores. Data moves between devices by JAX's collectives and lax.ppermute only.
A program may use at most 256 MiB of HBM per device.

v0:
```python
from functools import partial
import math
import jax
import jax.numpy as jnp
from jax import lax
from jax.sharding import PartitionSpec as P

HD = 128
NEGATIVE = -1000000000.0


def norm_rows(values, gain, shift):
    centre = jnp.mean(values, axis=-1, keepdims=True)
    centred = values - centre
    spread = jnp.mean(centred * centred, axis=-1, keepdims=True)
    return centred * lax.rsqrt(spread + 1e-05) * gain + shift


def on_path(query_pos, query_seg, key_pos, key_seg, parent):
    labels = jnp.arange(parent.shape[0], dtype=jnp.int32)
    first = jnp.sum(jnp.where(query_seg[:, None] == labels[None, :], parent[None, :], 0), axis=1)
    second = jnp.sum(jnp.where(first[:, None] == labels[None, :], parent[None, :], 0), axis=1)
    along = (
        (key_seg[None, :] == query_seg[:, None])
        | (key_seg[None, :] == first[:, None])
        | (key_seg[None, :] == second[:, None])
    )
    return along & (key_pos[None, :] <= query_pos[:, None])


def inner_rows(left, right):
    return lax.dot_general(
        left, right, (((0,), (0,)), ((), ())), preferred_element_type=jnp.float32
    )


def times_transposed(left, right):
    return lax.dot_general(
        left, right, (((1,), (1,)), ((), ())), preferred_element_type=jnp.float32
    )


def per_device(
    tokens,
    tree_position,
    segment,
    parent_table,
    norm1_gain,
    norm1_shift,
    query_weight,
    query_bias,
    key_weight,
    value_weight,
    value_bias,
    out_weight,
    out_bias,
    norm2_gain,
    norm2_shift,
    up_weight,
    up_bias,
    down_weight,
    down_bias,
    cotangent,
):
    w_query, w_key, w_value, w_out, w_up, w_down = (
        lax.all_gather(query_weight, "fsdp", axis=0, tiled=True),
        lax.all_gather(key_weight, "fsdp", axis=0, tiled=True),
        lax.all_gather(value_weight, "fsdp", axis=0, tiled=True),
        lax.all_gather(out_weight, "fsdp", axis=1, tiled=True),
        lax.all_gather(up_weight, "fsdp", axis=0, tiled=True),
        lax.all_gather(down_weight, "fsdp", axis=1, tiled=True),
    )
    key_position, key_segment = (
        lax.all_gather(tree_position, "ctx", axis=1, tiled=True),
        lax.all_gather(segment, "ctx", axis=1, tiled=True),
    )
    local_width = w_query.shape[1]
    head_count = local_width // HD
    score_scale = 1.0 / math.sqrt(HD)
    gelu_exact = partial(jax.nn.gelu, approximate=False)
    layer_rows = []
    input_grads = []
    running = [
        jnp.zeros(w_query.shape, jnp.float32),
        jnp.zeros(w_key.shape, jnp.float32),
        jnp.zeros(w_value.shape, jnp.float32),
        jnp.zeros(w_out.shape, jnp.float32),
        jnp.zeros(w_up.shape, jnp.float32),
        jnp.zeros(w_down.shape, jnp.float32),
        jnp.zeros(norm1_gain.shape, jnp.float32),
        jnp.zeros(norm1_shift.shape, jnp.float32),
        jnp.zeros(norm2_gain.shape, jnp.float32),
        jnp.zeros(norm2_shift.shape, jnp.float32),
        jnp.zeros(out_bias.shape, jnp.float32),
        jnp.zeros(down_bias.shape, jnp.float32),
    ]
    head_sums = [
        jnp.zeros(query_bias.shape, jnp.float32),
        jnp.zeros(value_bias.shape, jnp.float32),
        jnp.zeros(up_bias.shape, jnp.float32),
    ]
    for batch_index in range(tokens.shape[0]):
        inputs = tokens[batch_index].astype(jnp.float32)
        local_rows = inputs.shape[0]
        normed = norm_rows(inputs, norm1_gain, norm1_shift).astype(jnp.bfloat16)
        queries = (
            jnp.dot(normed, w_query, preferred_element_type=jnp.float32) + query_bias
        ).astype(jnp.bfloat16)
        keys_local = jnp.dot(normed, w_key, preferred_element_type=jnp.float32).astype(jnp.bfloat16)
        values_local = (
            jnp.dot(normed, w_value, preferred_element_type=jnp.float32) + value_bias
        ).astype(jnp.bfloat16)
        keys_tree, values_tree = (
            lax.all_gather(keys_local, "ctx", axis=0, tiled=True),
            lax.all_gather(values_local, "ctx", axis=0, tiled=True),
        )
        tree_rows = keys_tree.shape[0]
        visible = on_path(
            tree_position[batch_index],
            segment[batch_index],
            key_position[batch_index],
            key_segment[batch_index],
            parent_table[batch_index],
        )
        query_heads = queries.reshape(local_rows, head_count, HD)
        key_heads = keys_tree.reshape(tree_rows, head_count, HD)
        value_heads = values_tree.reshape(tree_rows, head_count, HD)
        scores = (
            jnp.einsum("qhd,khd->hqk", query_heads, key_heads, preferred_element_type=jnp.float32)
            * score_scale
        )
        scores = jnp.where(visible[None], scores, NEGATIVE)
        row_max = jnp.max(scores, axis=-1, keepdims=True)
        shifted = jnp.exp(scores - row_max)
        row_total = jnp.sum(shifted, axis=-1, keepdims=True)
        log_total = row_max + jnp.log(row_total)
        soft_low = (shifted / row_total).astype(jnp.bfloat16)
        attended = (
            jnp.einsum("hqk,khd->qhd", soft_low, value_heads, preferred_element_type=jnp.float32)
            .reshape(local_rows, local_width)
            .astype(jnp.bfloat16)
        )
        middle = inputs + (
            lax.psum(
                jnp.dot(attended, w_out, preferred_element_type=jnp.float32).astype(jnp.bfloat16),
                "tp",
            ).astype(jnp.float32)
            + out_bias
        )
        normed_mid = norm_rows(middle, norm2_gain, norm2_shift).astype(jnp.bfloat16)
        hidden = jnp.dot(normed_mid, w_up, preferred_element_type=jnp.float32) + up_bias
        active = gelu_exact(hidden).astype(jnp.bfloat16)
        result = middle + (
            lax.psum(
                jnp.dot(active, w_down, preferred_element_type=jnp.float32).astype(jnp.bfloat16),
                "tp",
            ).astype(jnp.float32)
            + down_bias
        )
        layer_rows.append(result.astype(jnp.bfloat16))
        grad_out = cotangent[batch_index]
        grad_float = grad_out.astype(jnp.float32)
        down_bias_term = jnp.sum(grad_float, axis=0)
        down_term = inner_rows(active, grad_out)
        _, gelu_pull = jax.vjp(gelu_exact, hidden)
        grad_hidden = gelu_pull(times_transposed(grad_out, w_down))[0].astype(jnp.bfloat16)
        up_bias_term = jnp.sum(grad_hidden.astype(jnp.float32), axis=0)
        up_term = inner_rows(normed_mid, grad_hidden)
        grad_normed_mid = lax.psum(
            times_transposed(grad_hidden, w_up).astype(jnp.bfloat16), "tp"
        ).astype(jnp.float32)
        _, second_pull = jax.vjp(norm_rows, middle, norm2_gain, norm2_shift)
        grad_mid_norm, second_gain_term, second_shift_term = second_pull(grad_normed_mid)
        grad_middle = grad_float + grad_mid_norm
        grad_branch = grad_middle.astype(jnp.bfloat16)
        out_bias_term = jnp.sum(grad_branch.astype(jnp.float32), axis=0)
        out_term = inner_rows(attended, grad_branch)
        grad_attended = times_transposed(grad_branch, w_out).astype(jnp.bfloat16)
        grad_heads = grad_attended.reshape(local_rows, head_count, HD)
        again = (
            jnp.einsum("qhd,khd->hqk", query_heads, key_heads, preferred_element_type=jnp.float32)
            * score_scale
        )
        again = jnp.where(visible[None], again, NEGATIVE)
        soft = jnp.exp(again - log_total)
        soft_again = soft.astype(jnp.bfloat16)
        grad_soft = jnp.einsum(
            "qhd,khd->hqk", grad_heads, value_heads, preferred_element_type=jnp.float32
        )
        inner = jnp.sum(soft * grad_soft, axis=-1, keepdims=True)
        grad_scores = (soft * (grad_soft - inner)).astype(jnp.bfloat16)
        grad_queries = (
            (
                jnp.einsum(
                    "hqk,khd->qhd", grad_scores, key_heads, preferred_element_type=jnp.float32
                )
                * score_scale
            )
            .reshape(local_rows, local_width)
            .astype(jnp.bfloat16)
        )
        key_part = (
            jnp.einsum("hqk,qhd->khd", grad_scores, query_heads, preferred_element_type=jnp.float32)
            * score_scale
        ).reshape(tree_rows, local_width)
        value_part = jnp.einsum(
            "hqk,qhd->khd", soft_again, grad_heads, preferred_element_type=jnp.float32
        ).reshape(tree_rows, local_width)
        grad_keys, grad_values = (
            lax.psum_scatter(
                key_part.astype(jnp.bfloat16), "ctx", scatter_dimension=0, tiled=True
            ).astype(jnp.float32),
            lax.psum_scatter(
                value_part.astype(jnp.bfloat16), "ctx", scatter_dimension=0, tiled=True
            ).astype(jnp.float32),
        )
        grad_keys = grad_keys.astype(jnp.bfloat16)
        grad_values = grad_values.astype(jnp.bfloat16)
        query_bias_term = jnp.sum(grad_queries.astype(jnp.float32), axis=0)
        value_bias_term = jnp.sum(grad_values.astype(jnp.float32), axis=0)
        query_term = inner_rows(normed, grad_queries)
        key_term = inner_rows(normed, grad_keys)
        value_term = inner_rows(normed, grad_values)
        grad_normed = lax.psum(
            (
                times_transposed(grad_queries, w_query)
                + times_transposed(grad_keys, w_key)
                + times_transposed(grad_values, w_value)
            ).astype(jnp.bfloat16),
            "tp",
        ).astype(jnp.float32)
        _, first_pull = jax.vjp(norm_rows, inputs, norm1_gain, norm1_shift)
        grad_in_norm, first_gain_term, first_shift_term = first_pull(grad_normed)
        input_grads.append((grad_middle + grad_in_norm).astype(jnp.bfloat16))
        head_sums = [
            head_sums[0] + query_bias_term,
            head_sums[1] + value_bias_term,
            head_sums[2] + up_bias_term,
        ]
        fresh = [
            query_term,
            key_term,
            value_term,
            out_term,
            up_term,
            down_term,
            first_gain_term,
            first_shift_term,
            second_gain_term,
            second_shift_term,
            out_bias_term,
            down_bias_term,
        ]
        running = [older + newer for older, newer in zip(running, fresh)]
    final = (
        lax.psum_scatter(
            running[0].astype(jnp.bfloat16), ("fsdp", "ctx"), scatter_dimension=0, tiled=True
        ).astype(jnp.float32),
        lax.psum_scatter(
            running[1].astype(jnp.bfloat16), ("fsdp", "ctx"), scatter_dimension=0, tiled=True
        ).astype(jnp.float32),
        lax.psum_scatter(
            running[2].astype(jnp.bfloat16), ("fsdp", "ctx"), scatter_dimension=0, tiled=True
        ).astype(jnp.float32),
        lax.psum_scatter(
            running[3].astype(jnp.bfloat16), ("fsdp", "ctx"), scatter_dimension=1, tiled=True
        ).astype(jnp.float32),
        lax.psum_scatter(
            running[4].astype(jnp.bfloat16), ("fsdp", "ctx"), scatter_dimension=0, tiled=True
        ).astype(jnp.float32),
        lax.psum_scatter(
            running[5].astype(jnp.bfloat16), ("fsdp", "ctx"), scatter_dimension=1, tiled=True
        ).astype(jnp.float32),
        lax.psum_scatter(
            running[6].astype(jnp.bfloat16), ("fsdp", "ctx"), scatter_dimension=0, tiled=True
        ).astype(jnp.float32),
        lax.psum_scatter(
            running[7].astype(jnp.bfloat16), ("fsdp", "ctx"), scatter_dimension=0, tiled=True
        ).astype(jnp.float32),
        lax.psum_scatter(
            running[8].astype(jnp.bfloat16), ("fsdp", "ctx"), scatter_dimension=0, tiled=True
        ).astype(jnp.float32),
        lax.psum_scatter(
            running[9].astype(jnp.bfloat16), ("fsdp", "ctx"), scatter_dimension=0, tiled=True
        ).astype(jnp.float32),
        lax.psum_scatter(
            running[10].astype(jnp.bfloat16), ("fsdp", "ctx"), scatter_dimension=0, tiled=True
        ).astype(jnp.float32),
        lax.psum_scatter(
            running[11].astype(jnp.bfloat16), ("fsdp", "ctx"), scatter_dimension=0, tiled=True
        ).astype(jnp.float32),
    )
    bias_totals = lax.psum((head_sums[0], head_sums[1], head_sums[2]), ("fsdp", "ctx"))
    return (
        jnp.stack(layer_rows),
        jnp.stack(input_grads),
        final[6],
        final[7],
        final[0],
        bias_totals[0],
        final[1],
        final[2],
        bias_totals[1],
        final[3],
        final[10],
        final[8],
        final[9],
        final[4],
        bias_totals[2],
        final[5],
        final[11],
    )


def solution(mesh):
    in_specs = (
        P("fsdp", "ctx", None),
        P("fsdp", "ctx"),
        P("fsdp", "ctx"),
        P("fsdp", None),
        P(),
        P(),
        P("fsdp", "tp"),
        P("tp"),
        P("fsdp", "tp"),
        P("fsdp", "tp"),
        P("tp"),
        P("tp", "fsdp"),
        P(),
        P(),
        P(),
        P("fsdp", "tp"),
        P("tp"),
        P("tp", "fsdp"),
        P(),
        P("fsdp", "ctx", None),
    )
    out_specs = (
        P("fsdp", "ctx", None),
        P("fsdp", "ctx", None),
        P(("fsdp", "ctx")),
        P(("fsdp", "ctx")),
        P(("fsdp", "ctx"), "tp"),
        P("tp"),
        P(("fsdp", "ctx"), "tp"),
        P(("fsdp", "ctx"), "tp"),
        P("tp"),
        P("tp", ("fsdp", "ctx")),
        P(("fsdp", "ctx")),
        P(("fsdp", "ctx")),
        P(("fsdp", "ctx")),
        P(("fsdp", "ctx"), "tp"),
        P("tp"),
        P("tp", ("fsdp", "ctx")),
        P(("fsdp", "ctx")),
    )
    return jax.shard_map(
        per_device, mesh=mesh, in_specs=in_specs, out_specs=out_specs, check_vma=False
    )
```

profile of v0, /device:TPU:0, one launch (start us, length us, event | category | flops | bytes accessed | tf_op | source)
XLA Modules:
  0.0 1765.6 jit_solution(16813001893812341595)
XLA Ops:
  14.5 30.9 %all-gather.17.cloned.1.call-done = bf16[2048,512]{1,0:T(8,128)(2,1)} async-done(((bf16[1024,512]{1,0:T(8,128)(2,1)}), bf16[2048,512]{1,0:T(8,128)(2,1)}) %all-gather.17.cloned.1.call-update) | async-done | bytes 2097168 | tf_op jit(solution)/shard_map/all_gather | solution.py:67
  49.2 30.9 %all-gather.11.cloned.1.call-done = bf16[2048,512]{1,0:T(8,128)(2,1)} async-done(((bf16[1024,512]{1,0:T(8,128)(2,1)}), bf16[2048,512]{1,0:T(8,128)(2,1)}) %all-gather.11.cloned.1.call-update) | async-done | bytes 2097168 | tf_op jit(solution)/shard_map/all_gather | solution.py:68
  84.4 13.3 all_gather.39
  97.6 13.4 all_gather.38
  118.4 44.0 %all-gather.19.cloned.1.call-done = bf16[2048,512]{1,0:T(8,128)(2,1)} async-done(((bf16[512,512]{1,0:T(8,128)(2,1)}), bf16[2048,512]{1,0:T(8,128)(2,1)}) %all-gather.19.cloned.1.call-update) | async-done | bytes 2097168 | tf_op jit(solution)/shard_map/all_gather | solution.py:114
  165.4 9.3 fusion.162
  174.7 8.2 fusion
  182.8 26.1 %all-gather.13.cloned.1.call-done = bf16[2048,512]{1,0:T(8,128)(2,1)} async-done(((bf16[512,512]{1,0:T(8,128)(2,1)}), bf16[2048,512]{1,0:T(8,128)(2,1)}) %all-gather.13.cloned.1.call-update) | async-done | bytes 2097168 | tf_op jit(solution)/shard_map/all_gather | solution.py:115
  208.9 8.5 fusion.127
  217.4 24.8 %all-gather.21.cloned.1.call-done = bf16[512,2048]{1,0:T(8,128)(2,1)} async-done(((bf16[512,1024]{1,0:T(8,128)(2,1)}), bf16[512,2048]{1,0:T(8,128)(2,1)}) %all-gather.21.cloned.1.call-update) | async-done | bytes 2097168 | tf_op jit(solution)/shard_map/all_gather | solution.py:69
  242.3 4.2 convolution_convert_fusion.5
  246.9 51.0 %all-reduce.15.cloned.1.call-done = bf16[512,2048]{1,0:T(8,128)(2,1)} async-done(((bf16[512,2048]{1,0:T(8,128)(2,1)}), bf16[512,2048]{1,0:T(8,128)(2,1)}) %all-reduce.15.cloned.1.call-update) | async-done | bytes 2097168 | tf_op jit(solution)/shard_map/psum | solution.py:144
  298.0 4.3 fusion.69
  312.4 4.8 fusion.123
  317.3 35.4 %all-gather.29.cloned.1.call-done = bf16[2048,512]{1,0:T(8,128)(2,1)} async-done(((bf16[512,512]{1,0:T(8,128)(2,1)}), bf16[2048,512]{1,0:T(8,128)(2,1)}) %all-gather.29.cloned.1.call-update) | async-done | bytes 2097168 | tf_op jit(solution)/shard_map/all_gather | solution.py:114
  355.6 9.5 fusion.163
  365.0 8.2 fusion.1
  373.2 26.0 %all-gather.27.cloned.1.call-done = bf16[2048,512]{1,0:T(8,128)(2,1)} async-done(((bf16[512,512]{1,0:T(8,128)(2,1)}), bf16[2048,512]{1,0:T(8,128)(2,1)}) %all-gather.27.cloned.1.call-update) | async-done | bytes 2097168 | tf_op jit(solution)/shard_map/all_gather | solution.py:115
  399.3 8.3 fusion.124
  412.6 48.8 %all-reduce.17.cloned.1.call-done = bf16[512,2048]{1,0:T(8,128)(2,1)} async-done(((bf16[512,2048]{1,0:T(8,128)(2,1)}), bf16[512,2048]{1,0:T(8,128)(2,1)}) %all-reduce.17.cloned.1.call-update) | async-done | bytes 2097168 | tf_op jit(solution)/shard_map/psum | solution.py:144
  461.4 4.5 multiply_reduce_fusion.3
  467.8 99.3 %all-gather.23.cloned.1.call-done = bf16[2048,2048]{1,0:T(8,128)(2,1)} async-done(((bf16[1024,2048]{1,0:T(8,128)(2,1)}), bf16[2048,2048]{1,0:T(8,128)(2,1)}) %all-gather.23.cloned.1.call-update) | async-done | bytes 8388624 | tf_op jit(solution)/shard_map/all_gather | solution.py:70
  567.1 8.0 fusion.142
  577.3 26.2 %multiply_convert_fusion.5 = (bf16[512,2048]{1,0:T(8,128)(2,1)}, f32[512,2048]{1,0:T(8,128)}, bf16[512,2048]{1,0:T(8,128)(2,1)}, f32[512,2048]{1,0:T(8,128)}, f32[512,2048]{1,0:T(8,128)}) fusion(f32[2048]{0:T(1024)S(1)} %copy-done.101, f32[512,2048]{1,0:T(8,128)S(1)} %fusion.142, bf16[2048,2048]{1,0:T(8,128)(2,1)S(1)} %copy-done.99, ...), kind=kOutput, calls=%fused_computation.131 | convolution fusion | flops 4442816512 | bytes 33591296 | tf_op jit(solution)/shard_map/dot_general | solution.py:151
  603.5 68.9 %all-gather.25.cloned.1.call-done = bf16[2048,2048]{1,0:T(8,128)(2,1)} async-done(((bf16[2048,1024]{1,0:T(8,128)(2,1)}), bf16[2048,2048]{1,0:T(8,128)(2,1)}) %all-gather.25.cloned.1.call-update) | async-done | bytes 8388624 | tf_op jit(solution)/shard_map/all_gather | solution.py:71
  672.5 14.2 convert_reduce_fusion.8
  686.6 10.0 convolution_convert_fusion
  696.6 12.2 convert_reduce_fusion.9
  708.8 9.9 convolution_convert_fusion.1
  719.4 85.0 %all-reduce.21.cloned.1.call-done = (bf16[512,2048]{1,0:T(8,128)(2,1)}, bf16[512,2048]{1,0:T(8,128)(2,1)}) async-done(((bf16[512,2048]{1,0:T(8,128)(2,1)}, bf16[512,2048]{1,0:T(8,128)(2,1)}), (bf16[512,2048]{1,0:T(8,128)(2,1)}, bf16[512,2048]{1,0:T(8,128)(2,1)})) %all-reduce.21.cloned.1.call-update) | async-done | bytes 4194320 | tf_op jit(solution)/shard_map/psum | solution.py:169
  804.4 6.9 fusion.37
  811.5 5.7 fusion.52
  817.3 8.8 convert_reduce_fusion.10
  829.6 4.4 fusion.70
  837.1 10.7 fusion.73
  847.9 11.3 multiply_reduce_fusion.1
  859.2 12.0 multiply_convert_fusion.1
  875.6 11.5 multiply_reduce_fusion
  887.1 11.9 multiply_convert_fusion
  908.5 6.6 convert_reduce_fusion.15
  916.7 6.4 convert_reduce_fusion.14
  926.2 4.4 fusion.169
  930.5 5.9 add_convert_fusion.3
  936.5 31.4 %reduce-scatter.11.cloned.1.call-done = bf16[512,512]{0,1:T(8,128)(2,1)} async-done(((bf16[2048,512]{0,1:T(8,128)(2,1)}), bf16[512,512]{0,1:T(8,128)(2,1)}) %reduce-scatter.11.cloned.1.call-update) | async-done | bytes 524304 | tf_op jit(solution)/shard_map/reduce_scatter | solution.py:210
  967.9 4.4 fusion.168
  972.3 40.7 %reduce-scatter.15.cloned.1.call-done = bf16[512,512]{0,1:T(8,128)(2,1)} async-done(((bf16[2048,512]{0,1:T(8,128)(2,1)}), bf16[512,512]{0,1:T(8,128)(2,1)}) %reduce-scatter.15.cloned.1.call-update) | async-done | bytes 524304 | tf_op jit(solution)/shard_map/reduce_scatter | solution.py:210
  1012.9 5.9 add_convert_fusion.4
  1019.1 9.2 convolution_convert_fusion.4
  1028.3 9.3 convolution_convert_fusion.2
  1049.6 13.8 fusion.140
  1063.4 15.7 add_convert_fusion.1
  1080.7 9.9 fusion.98
  1090.6 11.0 add_convert_fusion
  1108.8 46.7 %reduce-scatter.19.cloned.1.call-done = bf16[256,512]{1,0:T(8,128)(2,1)} async-done(((bf16[2048,512]{1,0:T(8,128)(2,1)}), bf16[256,512]{1,0:T(8,128)(2,1)}) %reduce-scatter.19.cloned.1.call-update) | async-done | bytes 262160 | tf_op jit(solution)/shard_map/reduce_scatter | solution.py:256
  1157.3 35.1 %all-reduce.6 = (f32[512]{0:T(512)}, f32[512]{0:T(512)}, f32[2048]{0:T(1024)}) all-reduce(f32[512]{0:T(512)S(1)} %add_bitcast_fusion, f32[512]{0:T(512)S(1)} %add.353, f32[2048]{0:T(1024)S(1)} %add.359), channel_id=1, replica_groups=mesh['fsdp'=2,'ctx'=4,'tp'=4] {'fsdp','ctx'}, use_global_device_ids=true, to_apply=%region_47.48 | all-reduce | flops 3072 | bytes 24576 | tf_op jit(solution)/shard_map/psum | solution.py:293
  1192.4 34.0 %reduce-scatter.23.cloned.1.call-done = bf16[256,512]{1,0:T(8,128)(2,1)} async-done(((bf16[2048,512]{1,0:T(8,128)(2,1)}), bf16[256,512]{1,0:T(8,128)(2,1)}) %reduce-scatter.23.cloned.1.call-update) | async-done | bytes 262160 | tf_op jit(solution)/shard_map/reduce_scatter | solution.py:262
  1228.2 69.2 %reduce-scatter.21.cloned.1.call-done = bf16[256,512]{1,0:T(8,128)(2,1)} async-done(((bf16[2048,512]{1,0:T(8,128)(2,1)}), bf16[256,512]{1,0:T(8,128)(2,1)}) %reduce-scatter.21.cloned.1.call-update) | async-done | bytes 262160 | tf_op jit(solution)/shard_map/reduce_scatter | solution.py:259
  1299.2 153.4 %all-reduce.19.cloned.1.call-done = (bf16[512,2048]{1,0:T(8,128)(2,1)}, bf16[512,2048]{1,0:T(8,128)(2,1)}, bf16[512,2048]{1,0:T(8,128)(2,1)}, bf16[512,2048]{1,0:T(8,128)(2,1)}) async-done(((bf16[512,2048]{1,0:T(8,128)(2,1)}, bf16[512,2048]{1,0:T(8,128)(2,1)}, bf16[512,2048]{1,0:T(8,128)(2,1)}, bf16[512,2048]{1,0:T(8,128)(2,1)}), (bf16[512,2048]{1,0:T(8,128)(2,1)}, bf16[512,2048]{1,0:T(8,128)(2,1)}, ...) | async-done | bytes 8388624 | tf_op jit(solution)/shard_map/psum | solution.py:154
  1452.6 4.7 fusion.41
  1462.6 40.6 %all-reduce.7 = (bf16[2048]{0:T(1024)(128)(2,1)S(1)}, bf16[2048]{0:T(1024)(128)(2,1)S(1)}, bf16[2048]{0:T(1024)(128)(2,1)S(1)}, bf16[2048]{0:T(1024)(128)(2,1)S(...) all-reduce(bf16[2048]{0:T(1024)(128)(2,1)S(1)} %add_convert_fusion., ...), channel_id=6, replica_groups=mesh['fsdp'=2,'ctx'=4,'tp'=4] {'fsdp','ctx'}, use_global_device_ids=true, to_apply=%region_40.41.clone | all-reduce | flops 12288 | bytes 49152
  1507.2 7.8 fusion.112
  1516.2 5.0 fusion.113
  1525.9 79.1 %reduce-scatter.27.cloned.1.call-done = bf16[256,2048]{1,0:T(8,128)(2,1)} async-done(((bf16[2048,2048]{1,0:T(8,128)(2,1)}), bf16[256,2048]{1,0:T(8,128)(2,1)}) %reduce-scatter.27.cloned.1.call-update) | async-done | bytes 1048592 | tf_op jit(solution)/shard_map/reduce_scatter | solution.py:268
  1607.9 147.7 %reduce-scatter.29.cloned.1.call-done = bf16[2048,256]{1,0:T(8,128)(2,1)} async-done(((bf16[2048,2048]{1,0:T(8,128)(2,1)}), bf16[2048,256]{1,0:T(8,128)(2,1)}) %reduce-scatter.29.cloned.1.call-update) | async-done | bytes 1048592 | tf_op jit(solution)/shard_map/reduce_scatter | solution.py:271
  (367 shorter events, 119.9 us)
Async XLA Ops:
  7.2 38.2 %all-gather.17.cloned.1.call-start = ((), (), s32[]{:S(2)}) async-start(), calls=%async_computation.13 | async-start | bytes 3145728 | tf_op jit(solution)/shard_map/all_gather | solution.py:67
  7.9 72.1 %all-gather.11.cloned.1.call-start = ((), (), s32[]{:S(2)}) async-start(), calls=%async_computation.10 | async-start | bytes 3145728 | tf_op jit(solution)/shard_map/all_gather | solution.py:68
  8.7 106.0 %all-gather.15.cloned.1.call-start = ((), (), s32[]{:S(2)}) async-start(), calls=%async_computation.12 | async-start | bytes 3145728 | tf_op jit(solution)/shard_map/all_gather | solution.py:66
  9.4 153.0 %all-gather.19.cloned.1.call-start = ((), (), s32[]{:S(2)}) async-start(), calls=%async_computation.14 | async-start | bytes 2621440 | tf_op jit(solution)/shard_map/all_gather | solution.py:114
  12.9 36.1 %copy-start.61 = (f32[512]{0:T(512)}, f32[512]{0:T(512)S(1)}, u32[]{:S(2)}) copy-start(f32[512]{0:T(512)S(1)} %broadcast_multiply_fusion.3) | copy-start | bytes 6148
  13.6 35.4 %copy-start.90 = (f32[512]{0:T(512)}, f32[512]{0:T(512)S(1)}, u32[]{:S(2)}) copy-start(f32[512]{0:T(512)S(1)} %fusion.40) | copy-start | bytes 6148
  13.7 35.4 %copy-start.68 = (f32[512]{0:T(512)}, f32[512]{0:T(512)S(1)}, u32[]{:S(2)}) copy-start(f32[512]{0:T(512)S(1)} %fusion.134) | copy-start | bytes 6148
  14.5 100.2 %copy-start.27 = (bf16[512,2048]{1,0:T(8,128)(2,1)}, bf16[512,2048]{1,0:T(8,128)(2,1)S(1)}, u32[]{:S(2)}) copy-start(bf16[512,2048]{1,0:T(8,128)(2,1)S(1)} %fusion.33) | copy-start | bytes 6291460
  14.5 65.5 %copy-start.104 = (f32[512]{0:T(512)S(1)}, f32[512]{0:T(512)}, u32[]{:S(2)}) copy-start(f32[512]{0:T(512)} %param.30) | copy-start | bytes 6148
  49.1 35.3 %copy-start.92 = (s32[2,512]{1,0:T(2,128)S(1)}, s32[2,512]{1,0:T(2,128)}, u32[]{:S(2)}) copy-start(s32[2,512]{1,0:T(2,128)} %param.21) | copy-start | bytes 12292
  49.1 48.6 %copy-start.93 = (s32[2,512]{1,0:T(2,128)S(1)}, s32[2,512]{1,0:T(2,128)}, u32[]{:S(2)}) copy-start(s32[2,512]{1,0:T(2,128)} %param.22) | copy-start | bytes 12292
  49.1 62.0 %copy-start.98 = (s32[2,7]{1,0:T(2,128)S(1)}, s32[2,7]{1,0:T(2,128)}, u32[]{:S(2)}) copy-start(s32[2,7]{1,0:T(2,128)} %param.23) | copy-start | bytes 172
  49.1 65.6 %copy-start.105 = (f32[512]{0:T(512)S(1)}, f32[512]{0:T(512)}, u32[]{:S(2)}) copy-start(f32[512]{0:T(512)} %param.27) | copy-start | bytes 6148
  49.1 159.8 %all-gather.13.cloned.1.call-start = ((), (), s32[]{:S(2)}) async-start(), calls=%async_computation.11 | async-start | bytes 2621440 | tf_op jit(solution)/shard_map/all_gather | solution.py:115
  83.7 158.5 %all-gather.21.cloned.1.call-start = ((), (), s32[]{:S(2)}) async-start(), calls=%async_computation.15 | async-start | bytes 3145728 | tf_op jit(solution)/shard_map/all_gather | solution.py:69
  84.3 213.7 %all-reduce.15.cloned.1.call-start = ((), (), s32[]{:S(2)}) async-start(), calls=%async_computation.16 | async-start | bytes 4194304 | tf_op jit(solution)/shard_map/psum | solution.py:144
  174.7 34.3 %copy-start.57 = (f32[4,512]{1,0:T(4,128)}, f32[4,512]{1,0:T(4,128)S(1)}, u32[]{:S(2)}) copy-start(f32[4,512]{1,0:T(4,128)S(1)} %get-tuple-element.86) | copy-start | bytes 24580
  182.8 34.6 %copy-start.66 = (f32[4,512]{1,0:T(4,128)}, f32[4,512]{1,0:T(4,128)S(1)}, u32[]{:S(2)}) copy-start(f32[4,512]{1,0:T(4,128)S(1)} %fusion) | copy-start | bytes 24580
  217.4 84.9 %copy-start.52 = (bf16[4,128,512]{2,1,0:T(8,128)(2,1)}, bf16[4,128,512]{2,1,0:T(8,128)(2,1)S(1)}, u32[]{:S(2)}) copy-start(bf16[4,128,512]{2,1,0:T(8,128)(2,1)S(1)} %fusion.127) | copy-start | bytes 1572868
  217.4 80.6 %copy-start.51 = (f32[2048]{0:T(1024)S(1)}, f32[2048]{0:T(1024)}, u32[]{:S(2)}) copy-start(f32[2048]{0:T(1024)} %param.32) | copy-start | bytes 24580
  246.5 106.1 %all-gather.29.cloned.1.call-start = ((), (), s32[]{:S(2)}) async-start(), calls=%async_computation.20 | async-start | bytes 2621440 | tf_op jit(solution)/shard_map/all_gather | solution.py:114
  246.9 65.5 %copy-start.63 = (f32[512]{0:T(512)}, f32[512]{0:T(512)S(1)}, u32[]{:S(2)}) copy-start(f32[512]{0:T(512)S(1)} %broadcast_multiply_fusion.1) | copy-start | bytes 6148
  306.7 92.5 %all-gather.27.cloned.1.call-start = ((), (), s32[]{:S(2)}) async-start(), calls=%async_computation.19 | async-start | bytes 2621440 | tf_op jit(solution)/shard_map/all_gather | solution.py:115
  310.5 150.9 %all-reduce.17.cloned.1.call-start = ((), (), s32[]{:S(2)}) async-start(), calls=%async_computation.21 | async-start | bytes 4194304 | tf_op jit(solution)/shard_map/psum | solution.py:144
  373.2 35.2 %copy-start.100 = (bf16[512,2048]{1,0:T(8,128)(2,1)S(1)}, bf16[512,2048]{1,0:T(8,128)(2,1)}, u32[]{:S(2)}) copy-start(bf16[512,2048]{1,0:T(8,128)(2,1)} %all-gather.21.cloned.1.call-done) | copy-start | bytes 6291460
  411.0 156.0 %all-gather.23.cloned.1.call-start = ((), (), s32[]{:S(2)}) async-start(), calls=%async_computation.17 | async-start | bytes 12582912 | tf_op jit(solution)/shard_map/all_gather | solution.py:70
  411.8 260.7 %all-gather.25.cloned.1.call-start = ((), (), s32[]{:S(2)}) async-start(), calls=%async_computation.18 | async-start | bytes 12582912 | tf_op jit(solution)/shard_map/all_gather | solution.py:71
  412.3 392.0 %all-reduce.21.cloned.1.call-start = ((), (), s32[]{:S(2)}) async-start(), calls=%async_computation.33 | async-start | bytes 8388608 | tf_op jit(solution)/shard_map/psum | solution.py:169
  465.9 101.2 %copy-start.56 = (f32[2048]{0:T(1024)S(1)}, f32[2048]{0:T(1024)}, u32[]{:S(2)}) copy-start(f32[2048]{0:T(1024)} %param.33) | copy-start | bytes 24580
  465.9 101.2 %copy-start.102 = (f32[2048]{0:T(1024)S(1)}, f32[2048]{0:T(1024)}, u32[]{:S(2)}) copy-start(f32[2048]{0:T(1024)} %param.34) | copy-start | bytes 24580
  465.9 351.3 %copy-start.59 = (f32[512]{0:T(512)}, f32[512]{0:T(512)S(1)}, u32[]{:S(2)}) copy-start(f32[512]{0:T(512)S(1)} %get-tuple-element.104) | copy-start | bytes 6148
  467.8 349.4 %copy-start.74 = (f32[512]{0:T(512)}, f32[512]{0:T(512)S(1)}, u32[]{:S(2)}) copy-start(f32[512]{0:T(512)S(1)} %fusion.137) | copy-start | bytes 6148
  467.8 109.5 %copy-start.101 = (f32[2048]{0:T(1024)S(1)}, f32[2048]{0:T(1024)}, u32[]{:S(2)}) copy-start(f32[2048]{0:T(1024)} %param.36) | copy-start | bytes 24580
  567.0 10.2 copy-start.3
  567.1 10.2 copy-start.13
  567.1 10.2 copy-start.99
  686.6 10.0 copy-start.16
  686.6 10.0 copy-start.110
  718.7 207.5 %reduce-scatter.13.cloned.1.call-start = ((), (), s32[]{:S(2)}) async-start(), calls=%async_computation.23 | async-start | bytes 2621440 | tf_op jit(solution)/shard_map/reduce_scatter | solution.py:213
  811.5 18.1 %slice-start = ((s8[16777216]{0:T(1024)(128)(4,1)}), s8[4194304]{0:T(1024)(128)(4,1)S(1)}, s32[]{:S(2)}) async-start(s8[16777216]{0:T(1024)(128)(4,1)} %bitcast.329), calls=%async_computation.34 | async-start | bytes 8388608
  811.5 18.1 %slice-start.1 = ((s8[16777216]{0:T(1024)(128)(4,1)}), s8[4194304]{0:T(1024)(128)(4,1)S(1)}, s32[]{:S(2)}) async-start(s8[16777216]{0:T(1024)(128)(4,1)} %bitcast.329), calls=%async_computation.35 | async-start | bytes 8388608
  817.3 12.3 slice-start.2
  817.3 12.3 slice-start.3
  834.0 96.5 %reduce-scatter.17.cloned.1.call-start = ((), (), s32[]{:S(2)}) async-start(), calls=%async_computation.25 | async-start | bytes 2621440 | tf_op jit(solution)/shard_map/reduce_scatter | solution.py:213
  837.1 10.8 copy-start.43
  847.8 120.1 %reduce-scatter.11.cloned.1.call-start = ((), (), s32[]{:S(2)}) async-start(), calls=%async_computation.22 | async-start | bytes 2621440 | tf_op jit(solution)/shard_map/reduce_scatter | solution.py:210
  859.2 12.0 copy-start.41
  875.5 137.4 %reduce-scatter.15.cloned.1.call-start = ((), (), s32[]{:S(2)}) async-start(), calls=%async_computation.24 | async-start | bytes 2621440 | tf_op jit(solution)/shard_map/reduce_scatter | solution.py:210
  887.1 12.0 copy-start.42
  903.5 203.5 %reduce-scatter.25.cloned.1.call-start = ((), (), s32[]{:S(2)}) async-start(), calls=%async_computation.29 | async-start | bytes 2359296 | tf_op jit(solution)/shard_map/reduce_scatter | solution.py:265
  908.0 247.5 %reduce-scatter.19.cloned.1.call-start = ((), (), s32[]{:S(2)}) async-start(), calls=%async_computation.26 | async-start | bytes 2359296 | tf_op jit(solution)/shard_map/reduce_scatter | solution.py:256
  926.1 300.4 %reduce-scatter.23.cloned.1.call-start = ((), (), s32[]{:S(2)}) async-start(), calls=%async_computation.28 | async-start | bytes 2359296 | tf_op jit(solution)/shard_map/reduce_scatter | solution.py:262
  936.5 361.0 %reduce-scatter.21.cloned.1.call-start = ((), (), s32[]{:S(2)}) async-start(), calls=%async_computation.27 | async-start | bytes 2359296 | tf_op jit(solution)/shard_map/reduce_scatter | solution.py:259
  972.3 46.8 %copy-start.107 = (bf16[512,2048]{1,0:T(8,128)(2,1)S(1)}, bf16[512,2048]{1,0:T(8,128)(2,1)}, u32[]{:S(2)}) copy-start(bf16[512,2048]{1,0:T(8,128)(2,1)} %get-tuple-element.64) | copy-start | bytes 6291460
  1018.8 433.8 %all-reduce.19.cloned.1.call-start = ((), (), s32[]{:S(2)}) async-start(), calls=%async_computation.32 | async-start | bytes 16777216 | tf_op jit(solution)/shard_map/psum | solution.py:154
  1048.9 14.5 copy-start.60
  1048.9 14.5 copy-start.75
  1048.9 556.1 %reduce-scatter.27.cloned.1.call-start = ((), (), s32[]{:S(2)}) async-start(), calls=%async_computation.30 | async-start | bytes 9437184 | tf_op jit(solution)/shard_map/reduce_scatter | solution.py:268
  1049.6 13.8 copy-start.6
  1079.1 676.5 %reduce-scatter.29.cloned.1.call-start = ((), (), s32[]{:S(2)}) async-start(), calls=%async_computation.31 | async-start | bytes 9437184 | tf_op jit(solution)/shard_map/reduce_scatter | solution.py:271
  1458.5 48.5 %copy-start.15 = (bf16[512,2048]{1,0:T(8,128)(2,1)S(1)}, bf16[512,2048]{1,0:T(8,128)(2,1)}, u32[]{:S(2)}) copy-start(bf16[512,2048]{1,0:T(8,128)(2,1)} %all-reduce.15.cloned.1.call-done) | copy-start | bytes 6291460
  1458.6 48.5 %copy-start.65 = (f32[2048]{0:T(1024)S(1)}, f32[2048]{0:T(1024)}, u32[]{:S(2)}) copy-start(f32[2048]{0:T(1024)} %param.38) | copy-start | bytes 24580
  1458.6 48.5 %copy-start.73 = (f32[512]{0:T(512)S(1)}, f32[512]{0:T(512)}, u32[]{:S(2)}) copy-start(f32[512]{0:T(512)} %copy-done.72) | copy-start | bytes 6148
  1458.6 48.5 %copy-start.89 = (f32[512]{0:T(512)S(1)}, f32[512]{0:T(512)}, u32[]{:S(2)}) copy-start(f32[512]{0:T(512)} %copy-done.88) | copy-start | bytes 6148
  (76 other events, 394.3 us)
Sparse Core Ops, SparseCore 0:
  9.5 35.8 all-gather.16
  46.9 33.0 all-gather.10
  81.6 33.0 all-gather.14
  116.7 45.6 all-gather.18
  164.4 44.4 all-gather.12
  210.3 31.8 all-gather.20
  246.6 51.3 all-reduce.14
  306.8 45.7 all-gather.28
  354.8 44.4 all-gather.26
  411.1 50.1 all-reduce.16
  462.9 104.0 all-gather.22
  568.4 103.9 all-gather.24
  718.8 85.5 all-reduce.20
  834.1 43.7 reduce-scatter.12
  880.1 42.8 reduce-scatter.16
  925.1 42.8 reduce-scatter.10
  970.1 42.8 reduce-scatter.14
  1016.3 68.1 reduce-scatter.24
  1088.0 67.4 reduce-scatter.18
  1158.9 67.5 reduce-scatter.22
  1230.0 67.3 reduce-scatter.20
  1300.7 151.8 all-reduce.18
  1456.2 148.7 reduce-scatter.26
  1608.6 146.9 reduce-scatter.28
where the time goes:
time: 1770 us
  waiting for transfers between devices  1180 us (67%)
  matrix products  317 us (18%)
  other arithmetic  126 us (7%)
  blocking collectives  102 us (6%)
  local copies, waits for them, and re-layouts  21.5 us (1%)
    psum x1, waiting for transfers between devices, per_device(): lax.psum(jnp.dot(active, w_down, preferred_element_type=jnp.float32).asty...  153 us
    reduce_scatter x1, waiting for transfers between devices, per_device(): lax.psum_scatter(running[5].astype(jnp.bfloat16), ('fsdp', 'ctx'), scatte...  148 us
    psum x2, waiting for transfers between devices, per_device(): lax.psum(jnp.dot(attended, w_out, preferred_element_type=jnp.float32).ast...  99.8 us
    all_gather x1, waiting for transfers between devices, per_device(): lax.all_gather(up_weight, 'fsdp', axis=0, tiled=True)  99.3 us
    psum x1, waiting for transfers between devices, per_device(): lax.psum(times_transposed(grad_hidden, w_up).astype(jnp.bfloat16), 'tp')  85 us
    all_gather x2, waiting for transfers between devices, per_device(): lax.all_gather(keys_local, 'ctx', axis=0, tiled=True)  79.4 us
    dot_general x12, matrix products, inner_rows(): lax.dot_general(left, right, (((0,), (0,)), ((), ())), preferred_element_...  79.2 us
    reduce_scatter x1, waiting for transfers between devices, per_device(): lax.psum_scatter(running[4].astype(jnp.bfloat16), ('fsdp', 'ctx'), scatte...  79.1 us
  transfers between devices with their start and end apart: 24, of which 21 were waited for; matrix products, arithmetic and copies ran while one was open for 20% of the time, Pallas kernels for 0%

commit v1 on v0

--- a/solution.py
+++ b/solution.py
@@ -7,6 +7,28 @@
 
 HD = 128
 NEGATIVE = -1000000000.0
+
+
+def joined_along(tiles, dim):
+    tiles = jnp.moveaxis(tiles, 0, dim)
+    shape = tiles.shape
+    return tiles.reshape(*shape[:dim], shape[dim] * shape[dim + 1], *shape[dim + 2 :])
+
+
+def grow_blocks(x, axis):
+    count = lax.axis_size(axis)
+    blocks = x[None]
+    for level in range(count.bit_length() - 1):
+        apart = 1 << level
+        theirs = lax.ppermute(blocks, axis, [(i, i ^ apart) for i in range(count)])
+        both = jnp.stack([blocks, theirs])
+        upper = lax.axis_index(axis) >> level & 1
+        blocks = jnp.where(upper == 0, both, both[::-1]).reshape(-1, *x.shape)
+    return blocks
+
+
+def collect(array, axis, dim):
+    return joined_along(grow_blocks(array, axis), dim)
 
 
 def norm_rows(values, gain, shift):
@@ -67,7 +89,7 @@
         lax.all_gather(key_weight, "fsdp", axis=0, tiled=True),
         lax.all_gather(value_weight, "fsdp", axis=0, tiled=True),
         lax.all_gather(out_weight, "fsdp", axis=1, tiled=True),
-        lax.all_gather(up_weight, "fsdp", axis=0, tiled=True),
+        collect(up_weight, "fsdp", 0),
         lax.all_gather(down_weight, "fsdp", axis=1, tiled=True),
     )
     key_position, key_segment = (

time: 1770 us -> 1660 us (0.938)
  waiting for transfers between devices: 1180 us -> 1050 us
  other arithmetic: 126 us -> 148 us
    all_gather x1 -> x0, waiting for transfers between devices: 99.3 us -> none  [per_device(): lax.all_gather(up_weight, 'fsdp', axis=0, tiled=True)]
    psum x2, waiting for transfers between devices: 99.8 us -> 78.3 us  [per_device(): lax.psum(jnp.dot(attended, w_out, preferred_element_type=jnp.float32).ast...]
  transfers between devices with their start and end apart: 24 -> 24, of which waited for: 21 -> 20; matrix products, arithmetic and copies ran while one was open for 20% -> 23% of each run, Pallas kernels for 0% -> 0%
where the time goes in v1:
time: 1660 us
  waiting for transfers between devices  1050 us (63%)
  matrix products  317 us (19%)
  other arithmetic  148 us (9%)
  blocking collectives  103 us (6%)
  local copies, waits for them, and re-layouts  21.3 us (1%)
  between operations  16.7 us (1%)
    psum x1, waiting for transfers between devices, per_device(): lax.psum(jnp.dot(active, w_down, preferred_element_type=jnp.float32).asty...  153 us
    reduce_scatter x1, waiting for transfers between devices, per_device(): lax.psum_scatter(running[5].astype(jnp.bfloat16), ('fsdp', 'ctx'), scatte...  148 us
    psum x1, waiting for transfers between devices, per_device(): lax.psum(times_transposed(grad_hidden, w_up).astype(jnp.bfloat16), 'tp')  85 us
    dot_general x12, matrix products, inner_rows(): lax.dot_general(left, right, (((0,), (0,)), ((), ())), preferred_element_...  79.2 us
    reduce_scatter x1, waiting for transfers between devices, per_device(): lax.psum_scatter(running[4].astype(jnp.bfloat16), ('fsdp', 'ctx'), scatte...  79.2 us
    psum x2, waiting for transfers between devices, per_device(): lax.psum(jnp.dot(attended, w_out, preferred_element_type=jnp.float32).ast...  78.3 us
    all_gather x2, waiting for transfers between devices, per_device(): lax.all_gather(keys_local, 'ctx', axis=0, tiled=True)  77.9 us
    reduce_scatter x2, waiting for transfers between devices, per_device(): lax.psum_scatter(key_part.astype(jnp.bfloat16), 'ctx', scatter_dimension=...  72 us
  transfers between devices with their start and end apart: 24, of which 20 were waited for; matrix products, arithmetic and copies ran while one was open for 23% of the time, Pallas kernels for 0%

profile of v1, /device:TPU:0, one launch (start us, length us, event | category | flops | bytes accessed | tf_op | source)
XLA Modules:
  0.0 1660.0 jit_solution(9006748655891074867)
XLA Ops:
  14.5 30.9 %all-gather.16.cloned.1.call-done = bf16[2048,512]{1,0:T(8,128)(2,1)} async-done(((bf16[1024,512]{1,0:T(8,128)(2,1)}), bf16[2048,512]{1,0:T(8,128)(2,1)}) %all-gather.16.cloned.1.call-update) | async-done | bytes 2097168 | tf_op jit(solution)/shard_map/all_gather | solution.py:89
  49.2 30.9 %all-gather.10.cloned.1.call-done = bf16[2048,512]{1,0:T(8,128)(2,1)} async-done(((bf16[1024,512]{1,0:T(8,128)(2,1)}), bf16[2048,512]{1,0:T(8,128)(2,1)}) %all-gather.10.cloned.1.call-update) | async-done | bytes 2097168 | tf_op jit(solution)/shard_map/all_gather | solution.py:90
  84.4 13.3 all_gather.36
  97.6 13.7 all_gather.35
  118.4 44.0 %all-gather.18.cloned.1.call-done = bf16[2048,512]{1,0:T(8,128)(2,1)} async-done(((bf16[512,512]{1,0:T(8,128)(2,1)}), bf16[2048,512]{1,0:T(8,128)(2,1)}) %all-gather.18.cloned.1.call-update) | async-done | bytes 2097168 | tf_op jit(solution)/shard_map/all_gather | solution.py:136
  165.4 9.3 fusion.162
  174.7 8.2 fusion
  182.8 26.1 %all-gather.12.cloned.1.call-done = bf16[2048,512]{1,0:T(8,128)(2,1)} async-done(((bf16[512,512]{1,0:T(8,128)(2,1)}), bf16[2048,512]{1,0:T(8,128)(2,1)}) %all-gather.12.cloned.1.call-update) | async-done | bytes 2097168 | tf_op jit(solution)/shard_map/all_gather | solution.py:137
  208.9 8.5 fusion.127
  217.4 24.8 %all-gather.20.cloned.1.call-done = bf16[512,2048]{1,0:T(8,128)(2,1)} async-done(((bf16[512,1024]{1,0:T(8,128)(2,1)}), bf16[512,2048]{1,0:T(8,128)(2,1)}) %all-gather.20.cloned.1.call-update) | async-done | bytes 2097168 | tf_op jit(solution)/shard_map/all_gather | solution.py:91
  246.7 51.3 %all-reduce.15.cloned.1.call-done = bf16[512,2048]{1,0:T(8,128)(2,1)} async-done(((bf16[512,2048]{1,0:T(8,128)(2,1)}), bf16[512,2048]{1,0:T(8,128)(2,1)}) %all-reduce.15.cloned.1.call-update) | async-done | bytes 2097168 | tf_op jit(solution)/shard_map/psum | solution.py:166
  298.0 4.3 fusion.69
  314.0 4.8 fusion.123
  318.8 33.9 %all-gather.26.cloned.1.call-done = bf16[2048,512]{1,0:T(8,128)(2,1)} async-done(((bf16[512,512]{1,0:T(8,128)(2,1)}), bf16[2048,512]{1,0:T(8,128)(2,1)}) %all-gather.26.cloned.1.call-update) | async-done | bytes 2097168 | tf_op jit(solution)/shard_map/all_gather | solution.py:136
  355.6 9.5 fusion.163
  365.1 8.2 fusion.1
  373.3 26.0 %all-gather.24.cloned.1.call-done = bf16[2048,512]{1,0:T(8,128)(2,1)} async-done(((bf16[512,512]{1,0:T(8,128)(2,1)}), bf16[2048,512]{1,0:T(8,128)(2,1)}) %all-gather.24.cloned.1.call-update) | async-done | bytes 2097168 | tf_op jit(solution)/shard_map/all_gather | solution.py:137
  399.3 8.3 fusion.124
  412.3 7.7 pad_maximum_fusion
  420.0 14.4 reverse_select_fusion
  434.4 27.1 %all-reduce.17.cloned.1.call-done = bf16[512,2048]{1,0:T(8,128)(2,1)} async-done(((bf16[512,2048]{1,0:T(8,128)(2,1)}), bf16[512,2048]{1,0:T(8,128)(2,1)}) %all-reduce.17.cloned.1.call-update) | async-done | bytes 2097168 | tf_op jit(solution)/shard_map/psum | solution.py:166
  461.5 4.5 multiply_reduce_fusion.3
  467.9 8.3 fusion.142
  478.1 26.2 %multiply_convert_fusion.5 = (bf16[512,2048]{1,0:T(8,128)(2,1)}, f32[512,2048]{1,0:T(8,128)}, bf16[512,2048]{1,0:T(8,128)(2,1)}, f32[512,2048]{1,0:T(8,128)}, f32[512,2048]{1,0:T(8,128)}) fusion(f32[2048]{0:T(1024)S(1)} %copy-done.103, f32[512,2048]{1,0:T(8,128)S(1)} %fusion.142, bf16[2048,2048]{1,0:T(8,128)(2,1)S(1)} %bitcast.344, ...), kind=kOutput, calls=%fused_computation.133 | convolution fusion | flops 4442816512 | bytes 33591296 | tf_op jit(solution)/shard_map/dot_general | solution.py:173
  504.3 62.8 %all-gather.22.cloned.1.call-done = bf16[2048,2048]{1,0:T(8,128)(2,1)} async-done(((bf16[2048,1024]{1,0:T(8,128)(2,1)}), bf16[2048,2048]{1,0:T(8,128)(2,1)}) %all-gather.22.cloned.1.call-update) | async-done | bytes 8388624 | tf_op jit(solution)/shard_map/all_gather | solution.py:93
  567.1 14.1 convert_reduce_fusion.8
  581.3 10.0 convolution_convert_fusion
  591.3 12.1 convert_reduce_fusion.9
  603.4 9.9 convolution_convert_fusion.1
  614.0 85.0 %all-reduce.21.cloned.1.call-done = (bf16[512,2048]{1,0:T(8,128)(2,1)}, bf16[512,2048]{1,0:T(8,128)(2,1)}) async-done(((bf16[512,2048]{1,0:T(8,128)(2,1)}, bf16[512,2048]{1,0:T(8,128)(2,1)}), (bf16[512,2048]{1,0:T(8,128)(2,1)}, bf16[512,2048]{1,0:T(8,128)(2,1)})) %all-reduce.21.cloned.1.call-update) | async-done | bytes 4194320 | tf_op jit(solution)/shard_map/psum | solution.py:191
  698.9 6.9 fusion.37
  706.1 5.7 fusion.52
  711.9 8.8 convert_reduce_fusion.10
  724.2 4.4 fusion.70
  731.8 10.6 fusion.73
  742.5 11.4 multiply_reduce_fusion.1
  753.9 12.0 multiply_convert_fusion.1
  770.2 11.6 multiply_reduce_fusion
  781.8 11.9 multiply_convert_fusion
  803.2 6.6 convert_reduce_fusion.15
  811.4 6.4 convert_reduce_fusion.14
  820.8 4.4 fusion.169
  825.2 5.9 add_convert_fusion.3
  831.2 31.4 %reduce-scatter.11.cloned.1.call-done = bf16[512,512]{0,1:T(8,128)(2,1)} async-done(((bf16[2048,512]{0,1:T(8,128)(2,1)}), bf16[512,512]{0,1:T(8,128)(2,1)}) %reduce-scatter.11.cloned.1.call-update) | async-done | bytes 524304 | tf_op jit(solution)/shard_map/reduce_scatter | solution.py:232
  862.6 4.4 fusion.168
  866.9 40.6 %reduce-scatter.15.cloned.1.call-done = bf16[512,512]{0,1:T(8,128)(2,1)} async-done(((bf16[2048,512]{0,1:T(8,128)(2,1)}), bf16[512,512]{0,1:T(8,128)(2,1)}) %reduce-scatter.15.cloned.1.call-update) | async-done | bytes 524304 | tf_op jit(solution)/shard_map/reduce_scatter | solution.py:232
  907.6 5.8 add_convert_fusion.4
  913.7 9.2 convolution_convert_fusion.4
  922.9 9.3 convolution_convert_fusion.2
  944.2 13.8 fusion.140
  957.9 15.7 add_convert_fusion.1
  975.3 9.9 fusion.98
  985.2 11.0 add_convert_fusion
  1003.4 46.5 %reduce-scatter.19.cloned.1.call-done = bf16[256,512]{1,0:T(8,128)(2,1)} async-done(((bf16[2048,512]{1,0:T(8,128)(2,1)}), bf16[256,512]{1,0:T(8,128)(2,1)}) %reduce-scatter.19.cloned.1.call-update) | async-done | bytes 262160 | tf_op jit(solution)/shard_map/reduce_scatter | solution.py:278
  1051.7 35.2 %all-reduce.6 = (f32[512]{0:T(512)}, f32[512]{0:T(512)}, f32[2048]{0:T(1024)}) all-reduce(f32[512]{0:T(512)S(1)} %add_bitcast_fusion, f32[512]{0:T(512)S(1)} %add.353, f32[2048]{0:T(1024)S(1)} %add.359), channel_id=1, replica_groups=mesh['fsdp'=2,'ctx'=4,'tp'=4] {'fsdp','ctx'}, use_global_device_ids=true, to_apply=%region_47.48 | all-reduce | flops 3072 | bytes 24576 | tf_op jit(solution)/shard_map/psum | solution.py:315
  1087.0 34.2 %reduce-scatter.23.cloned.1.call-done = bf16[256,512]{1,0:T(8,128)(2,1)} async-done(((bf16[2048,512]{1,0:T(8,128)(2,1)}), bf16[256,512]{1,0:T(8,128)(2,1)}) %reduce-scatter.23.cloned.1.call-update) | async-done | bytes 262160 | tf_op jit(solution)/shard_map/reduce_scatter | solution.py:284
  1123.0 69.0 %reduce-scatter.21.cloned.1.call-done = bf16[256,512]{1,0:T(8,128)(2,1)} async-done(((bf16[2048,512]{1,0:T(8,128)(2,1)}), bf16[256,512]{1,0:T(8,128)(2,1)}) %reduce-scatter.21.cloned.1.call-update) | async-done | bytes 262160 | tf_op jit(solution)/shard_map/reduce_scatter | solution.py:281
  1193.8 153.4 %all-reduce.19.cloned.1.call-done = (bf16[512,2048]{1,0:T(8,128)(2,1)}, bf16[512,2048]{1,0:T(8,128)(2,1)}, bf16[512,2048]{1,0:T(8,128)(2,1)}, bf16[512,2048]{1,0:T(8,128)(2,1)}) async-done(((bf16[512,2048]{1,0:T(8,128)(2,1)}, bf16[512,2048]{1,0:T(8,128)(2,1)}, bf16[512,2048]{1,0:T(8,128)(2,1)}, bf16[512,2048]{1,0:T(8,128)(2,1)}), (bf16[512,2048]{1,0:T(8,128)(2,1)}, bf16[512,2048]{1,0:T(8,128)(2,1)}, ...) | async-done | bytes 8388624 | tf_op jit(solution)/shard_map/psum | solution.py:176
  1347.2 4.7 fusion.41
  1357.2 40.6 %all-reduce.7 = (bf16[2048]{0:T(1024)(128)(2,1)S(1)}, bf16[2048]{0:T(1024)(128)(2,1)S(1)}, bf16[2048]{0:T(1024)(128)(2,1)S(1)}, bf16[2048]{0:T(1024)(128)(2,1)S(...) all-reduce(bf16[2048]{0:T(1024)(128)(2,1)S(1)} %add_convert_fusion., ...), channel_id=6, replica_groups=mesh['fsdp'=2,'ctx'=4,'tp'=4] {'fsdp','ctx'}, use_global_device_ids=true, to_apply=%region_40.41.clone | all-reduce | flops 12288 | bytes 49152
  1401.8 7.8 fusion.112
  1410.8 5.0 fusion.113
  1420.5 79.2 %reduce-scatter.27.cloned.1.call-done = bf16[256,2048]{1,0:T(8,128)(2,1)} async-done(((bf16[2048,2048]{1,0:T(8,128)(2,1)}), bf16[256,2048]{1,0:T(8,128)(2,1)}) %reduce-scatter.27.cloned.1.call-update) | async-done | bytes 1048592 | tf_op jit(solution)/shard_map/reduce_scatter | solution.py:290
  1502.5 147.9 %reduce-scatter.29.cloned.1.call-done = bf16[2048,256]{1,0:T(8,128)(2,1)} async-done(((bf16[2048,2048]{1,0:T(8,128)(2,1)}), bf16[2048,256]{1,0:T(8,128)(2,1)}) %reduce-scatter.29.cloned.1.call-update) | async-done | bytes 1048592 | tf_op jit(solution)/shard_map/reduce_scatter | solution.py:293
  (377 shorter events, 124.4 us)
Async XLA Ops:
  7.2 38.2 %all-gather.16.cloned.1.call-start = ((), (), s32[]{:S(2)}) async-start(), calls=%async_computation.13 | async-start | bytes 3145728 | tf_op jit(solution)/shard_map/all_gather | solution.py:89
  7.9 72.1 %all-gather.10.cloned.1.call-start = ((), (), s32[]{:S(2)}) async-start(), calls=%async_computation.10 | async-start | bytes 3145728 | tf_op jit(solution)/shard_map/all_gather | solution.py:90
  8.7 106.0 %all-gather.14.cloned.1.call-start = ((), (), s32[]{:S(2)}) async-start(), calls=%async_computation.12 | async-start | bytes 3145728 | tf_op jit(solution)/shard_map/all_gather | solution.py:88
  9.4 153.0 %all-gather.18.cloned.1.call-start = ((), (), s32[]{:S(2)}) async-start(), calls=%async_computation.14 | async-start | bytes 2621440 | tf_op jit(solution)/shard_map/all_gather | solution.py:136
  12.9 36.1 %copy-start.62 = (f32[512]{0:T(512)}, f32[512]{0:T(512)S(1)}, u32[]{:S(2)}) copy-start(f32[512]{0:T(512)S(1)} %broadcast_multiply_fusion.3) | copy-start | bytes 6148
  13.6 35.4 %copy-start.93 = (f32[512]{0:T(512)}, f32[512]{0:T(512)S(1)}, u32[]{:S(2)}) copy-start(f32[512]{0:T(512)S(1)} %fusion.40) | copy-start | bytes 6148
  13.7 35.4 %copy-start.71 = (f32[512]{0:T(512)}, f32[512]{0:T(512)S(1)}, u32[]{:S(2)}) copy-start(f32[512]{0:T(512)S(1)} %fusion.134) | copy-start | bytes 6148
  14.5 100.2 %copy-start.26 = (bf16[512,2048]{1,0:T(8,128)(2,1)}, bf16[512,2048]{1,0:T(8,128)(2,1)S(1)}, u32[]{:S(2)}) copy-start(bf16[512,2048]{1,0:T(8,128)(2,1)S(1)} %fusion.33) | copy-start | bytes 6291460
  14.5 65.5 %copy-start.106 = (f32[512]{0:T(512)S(1)}, f32[512]{0:T(512)}, u32[]{:S(2)}) copy-start(f32[512]{0:T(512)} %param.30) | copy-start | bytes 6148
  49.1 35.3 %copy-start.95 = (s32[2,512]{1,0:T(2,128)S(1)}, s32[2,512]{1,0:T(2,128)}, u32[]{:S(2)}) copy-start(s32[2,512]{1,0:T(2,128)} %param.21) | copy-start | bytes 12292
  49.1 48.6 %copy-start.96 = (s32[2,512]{1,0:T(2,128)S(1)}, s32[2,512]{1,0:T(2,128)}, u32[]{:S(2)}) copy-start(s32[2,512]{1,0:T(2,128)} %param.22) | copy-start | bytes 12292
  49.1 62.3 %copy-start.101 = (s32[2,7]{1,0:T(2,128)S(1)}, s32[2,7]{1,0:T(2,128)}, u32[]{:S(2)}) copy-start(s32[2,7]{1,0:T(2,128)} %param.23) | copy-start | bytes 172
  49.1 65.6 %copy-start.107 = (f32[512]{0:T(512)S(1)}, f32[512]{0:T(512)}, u32[]{:S(2)}) copy-start(f32[512]{0:T(512)} %param.27) | copy-start | bytes 6148
  49.1 159.8 %all-gather.12.cloned.1.call-start = ((), (), s32[]{:S(2)}) async-start(), calls=%async_computation.11 | async-start | bytes 2621440 | tf_op jit(solution)/shard_map/all_gather | solution.py:137
  83.7 158.5 %all-gather.20.cloned.1.call-start = ((), (), s32[]{:S(2)}) async-start(), calls=%async_computation.15 | async-start | bytes 3145728 | tf_op jit(solution)/shard_map/all_gather | solution.py:91
  84.3 213.7 %all-reduce.15.cloned.1.call-start = ((), (), s32[]{:S(2)}) async-start(), calls=%async_computation.16 | async-start | bytes 4194304 | tf_op jit(solution)/shard_map/psum | solution.py:166
  174.7 34.2 %copy-start.56 = (f32[4,512]{1,0:T(4,128)}, f32[4,512]{1,0:T(4,128)S(1)}, u32[]{:S(2)}) copy-start(f32[4,512]{1,0:T(4,128)S(1)} %get-tuple-element.86) | copy-start | bytes 24580
  182.8 34.5 %copy-start.67 = (f32[4,512]{1,0:T(4,128)}, f32[4,512]{1,0:T(4,128)S(1)}, u32[]{:S(2)}) copy-start(f32[4,512]{1,0:T(4,128)S(1)} %fusion) | copy-start | bytes 24580
  217.4 84.9 %copy-start.51 = (bf16[4,128,512]{2,1,0:T(8,128)(2,1)}, bf16[4,128,512]{2,1,0:T(8,128)(2,1)S(1)}, u32[]{:S(2)}) copy-start(bf16[4,128,512]{2,1,0:T(8,128)(2,1)S(1)} %fusion.127) | copy-start | bytes 1572868
  217.4 80.6 %copy-start.50 = (f32[2048]{0:T(1024)S(1)}, f32[2048]{0:T(1024)}, u32[]{:S(2)}) copy-start(f32[2048]{0:T(1024)} %param.32) | copy-start | bytes 24580
  246.5 106.2 %all-gather.26.cloned.1.call-start = ((), (), s32[]{:S(2)}) async-start(), calls=%async_computation.19 | async-start | bytes 2621440 | tf_op jit(solution)/shard_map/all_gather | solution.py:136
  246.7 67.3 %copy-start.64 = (f32[512]{0:T(512)}, f32[512]{0:T(512)S(1)}, u32[]{:S(2)}) copy-start(f32[512]{0:T(512)S(1)} %broadcast_multiply_fusion.1) | copy-start | bytes 6148
  302.9 11.1 copy-start.87
  306.8 92.6 %all-gather.24.cloned.1.call-start = ((), (), s32[]{:S(2)}) async-start(), calls=%async_computation.18 | async-start | bytes 2621440 | tf_op jit(solution)/shard_map/all_gather | solution.py:137
  310.5 150.9 %all-reduce.17.cloned.1.call-start = ((), (), s32[]{:S(2)}) async-start(), calls=%async_computation.20 | async-start | bytes 4194304 | tf_op jit(solution)/shard_map/psum | solution.py:166
  310.6 101.7 %collective-permute-start = (bf16[1,1024,2048]{2,1,0:T(8,128)(2,1)}, bf16[1,1024,2048]{2,1,0:T(8,128)(2,1)}, u32[]{:S(2)}, u32[]{:S(2)}) collective-permute-start(bf16[1,1024,2048]{2,1,0:T(8,128)(2,1)} %bitcast.353), channel_id=1, source_target_pairs={{0,16},{16,0},{1,17},{17,1},{2,18},{18,2},{3,19},{19,3},{4,20},{20... | collective-permute-start | bytes 12582920 | tf_op jit(solution)/shard_map/ppermute | solution.py:23
  365.1 34.2 %copy-start.58 = (f32[4,512]{1,0:T(4,128)}, f32[4,512]{1,0:T(4,128)S(1)}, u32[]{:S(2)}) copy-start(f32[4,512]{1,0:T(4,128)S(1)} %get-tuple-element.88) | copy-start | bytes 24580
  373.3 34.4 %copy-start.69 = (f32[4,512]{1,0:T(4,128)}, f32[4,512]{1,0:T(4,128)S(1)}, u32[]{:S(2)}) copy-start(f32[4,512]{1,0:T(4,128)S(1)} %fusion.1) | copy-start | bytes 24580
  373.3 35.2 %copy-start.102 = (bf16[512,2048]{1,0:T(8,128)(2,1)S(1)}, bf16[512,2048]{1,0:T(8,128)(2,1)}, u32[]{:S(2)}) copy-start(bf16[512,2048]{1,0:T(8,128)(2,1)} %all-gather.20.cloned.1.call-done) | copy-start | bytes 6291460
  411.1 156.0 %all-gather.22.cloned.1.call-start = ((), (), s32[]{:S(2)}) async-start(), calls=%async_computation.17 | async-start | bytes 12582912 | tf_op jit(solution)/shard_map/all_gather | solution.py:93
  411.9 287.1 %all-reduce.21.cloned.1.call-start = ((), (), s32[]{:S(2)}) async-start(), calls=%async_computation.32 | async-start | bytes 8388608 | tf_op jit(solution)/shard_map/psum | solution.py:191
  466.0 245.8 %copy-start.60 = (f32[512]{0:T(512)}, f32[512]{0:T(512)S(1)}, u32[]{:S(2)}) copy-start(f32[512]{0:T(512)S(1)} %get-tuple-element.104) | copy-start | bytes 6148
  466.8 11.3 slice-start.4
  467.9 243.9 %copy-start.77 = (f32[512]{0:T(512)}, f32[512]{0:T(512)S(1)}, u32[]{:S(2)}) copy-start(f32[512]{0:T(512)S(1)} %fusion.137) | copy-start | bytes 6148
  467.9 10.2 copy-start.12
  467.9 10.2 slice-start.5
  467.9 10.2 copy-start.103
  581.3 10.0 copy-start.112
  613.3 207.6 %reduce-scatter.13.cloned.1.call-start = ((), (), s32[]{:S(2)}) async-start(), calls=%async_computation.22 | async-start | bytes 2621440 | tf_op jit(solution)/shard_map/reduce_scatter | solution.py:235
  706.1 18.1 %slice-start = ((s8[16777216]{0:T(1024)(128)(4,1)}), s8[4194304]{0:T(1024)(128)(4,1)S(1)}, s32[]{:S(2)}) async-start(s8[16777216]{0:T(1024)(128)(4,1)} %bitcast.333), calls=%async_computation.33 | async-start | bytes 8388608
  706.1 18.1 %slice-start.1 = ((s8[16777216]{0:T(1024)(128)(4,1)}), s8[4194304]{0:T(1024)(128)(4,1)S(1)}, s32[]{:S(2)}) async-start(s8[16777216]{0:T(1024)(128)(4,1)} %bitcast.333), calls=%async_computation.34 | async-start | bytes 8388608
  711.8 12.3 slice-start.2
  711.9 12.3 slice-start.3
  728.6 96.6 %reduce-scatter.17.cloned.1.call-start = ((), (), s32[]{:S(2)}) async-start(), calls=%async_computation.24 | async-start | bytes 2621440 | tf_op jit(solution)/shard_map/reduce_scatter | solution.py:235
  731.8 10.7 copy-start.42
  742.4 120.1 %reduce-scatter.11.cloned.1.call-start = ((), (), s32[]{:S(2)}) async-start(), calls=%async_computation.21 | async-start | bytes 2621440 | tf_op jit(solution)/shard_map/reduce_scatter | solution.py:232
  753.9 12.0 copy-start.40
  770.2 137.4 %reduce-scatter.15.cloned.1.call-start = ((), (), s32[]{:S(2)}) async-start(), calls=%async_computation.23 | async-start | bytes 2621440 | tf_op jit(solution)/shard_map/reduce_scatter | solution.py:232
  781.8 12.0 copy-start.41
  798.2 203.4 %reduce-scatter.25.cloned.1.call-start = ((), (), s32[]{:S(2)}) async-start(), calls=%async_computation.28 | async-start | bytes 2359296 | tf_op jit(solution)/shard_map/reduce_scatter | solution.py:287
  802.8 247.2 %reduce-scatter.19.cloned.1.call-start = ((), (), s32[]{:S(2)}) async-start(), calls=%async_computation.25 | async-start | bytes 2359296 | tf_op jit(solution)/shard_map/reduce_scatter | solution.py:278
  820.8 300.4 %reduce-scatter.23.cloned.1.call-start = ((), (), s32[]{:S(2)}) async-start(), calls=%async_computation.27 | async-start | bytes 2359296 | tf_op jit(solution)/shard_map/reduce_scatter | solution.py:284
  831.1 360.9 %reduce-scatter.21.cloned.1.call-start = ((), (), s32[]{:S(2)}) async-start(), calls=%async_computation.26 | async-start | bytes 2359296 | tf_op jit(solution)/shard_map/reduce_scatter | solution.py:281
  866.9 46.7 %copy-start.109 = (bf16[512,2048]{1,0:T(8,128)(2,1)S(1)}, bf16[512,2048]{1,0:T(8,128)(2,1)}, u32[]{:S(2)}) copy-start(bf16[512,2048]{1,0:T(8,128)(2,1)} %get-tuple-element.64) | copy-start | bytes 6291460
  913.4 433.7 %all-reduce.19.cloned.1.call-start = ((), (), s32[]{:S(2)}) async-start(), calls=%async_computation.31 | async-start | bytes 16777216 | tf_op jit(solution)/shard_map/psum | solution.py:176
  943.5 14.4 copy-start.61
  943.5 14.4 copy-start.78
  943.5 556.2 %reduce-scatter.27.cloned.1.call-start = ((), (), s32[]{:S(2)}) async-start(), calls=%async_computation.29 | async-start | bytes 9437184 | tf_op jit(solution)/shard_map/reduce_scatter | solution.py:290
  944.2 13.8 copy-start.5
  973.7 676.6 %reduce-scatter.29.cloned.1.call-start = ((), (), s32[]{:S(2)}) async-start(), calls=%async_computation.30 | async-start | bytes 9437184 | tf_op jit(solution)/shard_map/reduce_scatter | solution.py:293
  1353.1 48.5 %copy-start.14 = (bf16[512,2048]{1,0:T(8,128)(2,1)S(1)}, bf16[512,2048]{1,0:T(8,128)(2,1)}, u32[]{:S(2)}) copy-start(bf16[512,2048]{1,0:T(8,128)(2,1)} %all-reduce.15.cloned.1.call-done) | copy-start | bytes 6291460
  1353.1 48.5 %copy-start.66 = (f32[2048]{0:T(1024)S(1)}, f32[2048]{0:T(1024)}, u32[]{:S(2)}) copy-start(f32[2048]{0:T(1024)} %param.38) | copy-start | bytes 24580
  1353.1 48.5 %copy-start.76 = (f32[512]{0:T(512)S(1)}, f32[512]{0:T(512)}, u32[]{:S(2)}) copy-start(f32[512]{0:T(512)} %copy-done.75) | copy-start | bytes 6148
  1353.1 48.5 %copy-start.92 = (f32[512]{0:T(512)S(1)}, f32[512]{0:T(512)}, u32[]{:S(2)}) copy-start(f32[512]{0:T(512)} %copy-done.91) | copy-start | bytes 6148
  (80 other events, 407.7 us)
Sparse Core Ops, SparseCore 0:
  9.5 35.8 all-gather.15
  46.9 33.0 all-gather.9
  81.6 33.0 all-gather.13
  116.7 45.6 all-gather.17
  164.4 44.4 all-gather.11
  210.3 31.8 all-gather.19
  246.6 51.3 all-reduce.14
  306.9 45.7 all-gather.25
  354.8 44.4 all-gather.23
  411.2 50.1 all-reduce.16
  463.0 104.0 all-gather.21
  613.4 85.5 all-reduce.20
  728.7 43.7 reduce-scatter.12
  774.7 42.8 reduce-scatter.16
  819.7 42.8 reduce-scatter.10
  864.7 42.8 reduce-scatter.14
  911.0 68.1 reduce-scatter.24
  982.5 67.3 reduce-scatter.18
  1053.4 67.6 reduce-scatter.22
  1124.5 67.3 reduce-scatter.20
  1195.3 151.8 all-reduce.18
  1350.8 148.8 reduce-scatter.26
  1503.3 146.9 reduce-scatter.28
